TPU v7x, 128 devices: a whole 4x4x4 slice. The times are simulated.
128 devices in a mesh: seq: 32 (over x, y, core), head: 4 (over z).
Axes of the slice: x: 4, y: 4, z: 4, core: 2. Of those that a mesh axis runs over, the one named last changes fastest.
Arguments:
- inputs: bfloat16 [32768, 1024], P('seq'), may hold values from -12 to 12
- latents: bfloat16 [2048, 1024], replicated, may hold values from -240 to 240
- query_weight: bfloat16 [1024, 1024], P(None, 'head'), may hold values from -1 to 1
- key_weight: bfloat16 [1024, 1024], P(None, 'head'), may hold values from -1 to 1
- value_weight: bfloat16 [1024, 1024], P(None, 'head'), may hold values from -0.1875 to 0.1875
- out_weight: bfloat16 [1024, 1024], P('head'), may hold values from -0.1875 to 0.1875
- prefix_lengths: int32 [2048], replicated, may hold values from 1 to 32768, as said below
- grad_out: bfloat16 [2048, 1024], P('seq', 'head'), may hold values from -6 to 6
Outputs:
- attention_out: bfloat16 [2048, 1024], P('seq', 'head')
- input_grad: bfloat16 [32768, 1024], P(('seq', 'head'))
- latent_grad: bfloat16 [2048, 1024], P('seq', 'head')
- query_weight_grad: float32 [1024, 1024], P('seq', 'head')
- key_weight_grad: float32 [1024, 1024], P('seq', 'head')
- value_weight_grad: float32 [1024, 1024], P('seq', 'head')
- out_weight_grad: float32 [1024, 1024], P('head', 'seq')
Inputs may be any that keep to these rules, and one draw needn't show every extreme that they name: `prefix_lengths`: nondecreasing in the latent index; the first is 1 and the last is 32768; all others are 2 or more.
All inputs are finite; a program needn't handle non-finite values.
Results may differ from a plain program's by a relative error of at most 0.012.
Values may be sent and summed in bfloat16 or wider, within the bound.
A program may use at most 128 MiB of HBM per device.

v0:
```python
import jax
import jax.numpy as jnp
from jax import lax
from jax.sharding import PartitionSpec as P

DH = 64


floor_value = -1e30


def on_device(
    inputs, latents, query_weight, key_weight, value_weight, out_weight, prefix_lengths, grad_out
):
    row_count = inputs.shape[0]
    latent_count = latents.shape[0]
    col_count = query_weight.shape[1]
    head_count = col_count // DH
    seq_count = lax.axis_size("seq")
    seq_index = lax.axis_index("seq")
    own_latents = latent_count // seq_count
    scaling = DH ** (-0.5)
    queries = (
        jnp.dot(latents, query_weight, preferred_element_type=jnp.float32)
        .astype(jnp.bfloat16)
        .reshape(latent_count, head_count, DH)
    )
    key_rows = jnp.dot(inputs, key_weight, preferred_element_type=jnp.float32).astype(jnp.bfloat16)
    value_rows = jnp.dot(inputs, value_weight, preferred_element_type=jnp.float32).astype(
        jnp.bfloat16
    )
    positions = seq_index * row_count + jnp.arange(row_count, dtype=jnp.int32)
    keys_split = key_rows.reshape(row_count, head_count, DH)
    values_split = value_rows.reshape(row_count, head_count, DH)
    key_tile = min(512, row_count)
    query_tile = min(512, latent_count)
    tile_count = row_count // key_tile
    block_count = latent_count // query_tile
    tile_least = positions.reshape(tile_count, key_tile).min(axis=1)
    block_most = prefix_lengths.reshape(block_count, query_tile).max(axis=1)

    def tile_data(tile_id):
        offset = tile_id * key_tile
        return (
            lax.dynamic_slice_in_dim(keys_split, offset, key_tile, 0),
            lax.dynamic_slice_in_dim(values_split, offset, key_tile, 0),
            lax.dynamic_slice_in_dim(positions, offset, key_tile, 0),
        )

    def scores_of(block_query, block_prefix, tile_keys, tile_pos):
        scores = (
            jnp.einsum("qhd,khd->hqk", block_query, tile_keys, preferred_element_type=jnp.float32)
            * scaling
        )
        visible = tile_pos[None, None, :] < block_prefix[None, :, None]
        return (scores, visible)

    def sweep(block_id, update, init):

        def visit(tile_id, state):
            return lax.cond(
                block_most[block_id] > tile_least[tile_id],
                lambda inner_state: update(tile_id, inner_state),
                lambda inner_state: inner_state,
                state,
            )

        return lax.fori_loop(0, tile_count, visit, init)

    maxima = []
    for block_id in range(block_count):
        block_query = queries[block_id * query_tile : (block_id + 1) * query_tile]
        block_prefix = prefix_lengths[block_id * query_tile : (block_id + 1) * query_tile]

        def update_max(tile_id, state, block_query=block_query, block_prefix=block_prefix):
            tile_keys, tile_values, tile_pos = tile_data(tile_id)
            scores, visible = scores_of(block_query, block_prefix, tile_keys, tile_pos)
            return jnp.maximum(state, jnp.where(visible, scores, floor_value).max(axis=2))

        maxima.append(
            sweep(
                block_id, update_max, jnp.full((head_count, query_tile), floor_value, jnp.float32)
            )
        )
    row_top = lax.pmax(jnp.concatenate(maxima, axis=1), "seq")
    totals = []
    partials = []
    for block_id in range(block_count):
        block_query = queries[block_id * query_tile : (block_id + 1) * query_tile]
        block_prefix = prefix_lengths[block_id * query_tile : (block_id + 1) * query_tile]
        block_top = row_top[:, block_id * query_tile : (block_id + 1) * query_tile]

        def update_sum(
            tile_id, state, block_query=block_query, block_prefix=block_prefix, block_top=block_top
        ):
            tile_keys, tile_values, tile_pos = tile_data(tile_id)
            scores, visible = scores_of(block_query, block_prefix, tile_keys, tile_pos)
            weights = jnp.where(visible, jnp.exp(scores - block_top[:, :, None]), 0.0)
            weighted = jnp.einsum(
                "hqk,khd->qhd",
                weights.astype(jnp.bfloat16),
                tile_values,
                preferred_element_type=jnp.float32,
            )
            return (state[0] + weights.sum(axis=2), state[1] + weighted)

        start_state = (
            jnp.zeros((head_count, query_tile), jnp.float32),
            jnp.zeros((query_tile, head_count, DH), jnp.float32),
        )
        block_sum, block_weighted = sweep(block_id, update_sum, start_state)
        totals.append(block_sum)
        partials.append(block_weighted)
    exp_total = jnp.concatenate(totals, axis=1).T
    weighted_sum = jnp.concatenate(partials, axis=0).reshape(latent_count, col_count)
    exp_all, weighted_all = lax.psum((exp_total, weighted_sum), "seq")
    attended = (
        (weighted_all.reshape(latent_count, head_count, DH) / exp_all[:, :, None])
        .astype(jnp.bfloat16)
        .reshape(latent_count, col_count)
    )
    own_attended = lax.dynamic_slice_in_dim(attended, seq_index * own_latents, own_latents, 0)
    attention_out = lax.psum_scatter(
        jnp.dot(own_attended, out_weight, preferred_element_type=jnp.float32),
        "head",
        scatter_dimension=1,
        tiled=True,
    ).astype(jnp.bfloat16)
    grad_rows = lax.all_gather(grad_out, "head", axis=1, tiled=True)
    dout_rows = jnp.dot(grad_rows, out_weight.T, preferred_element_type=jnp.float32).astype(
        jnp.bfloat16
    )
    out_weight_grad = lax.psum_scatter(
        jnp.dot(own_attended.T, grad_rows, preferred_element_type=jnp.float32),
        "seq",
        scatter_dimension=1,
        tiled=True,
    )
    dout = lax.all_gather(dout_rows, "seq", axis=0, tiled=True)
    inner = jnp.sum(
        dout.astype(jnp.float32).reshape(latent_count, head_count, DH)
        * attended.astype(jnp.float32).reshape(latent_count, head_count, DH),
        axis=2,
    )
    query_blocks = []
    key_grad = jnp.zeros((row_count, head_count, DH), jnp.float32)
    value_grad = jnp.zeros((row_count, head_count, DH), jnp.float32)
    for block_id in range(block_count):
        lower = block_id * query_tile
        upper = lower + query_tile
        block_query = queries[lower:upper]
        block_prefix = prefix_lengths[lower:upper]
        block_top = row_top[:, lower:upper]
        block_total = exp_all[lower:upper].T
        block_inner = inner[lower:upper].T
        block_dout = dout[lower:upper].reshape(query_tile, head_count, DH)

        def update_grad(
            tile_id,
            state,
            block_query=block_query,
            block_prefix=block_prefix,
            block_top=block_top,
            block_total=block_total,
            block_inner=block_inner,
            block_dout=block_dout,
        ):
            query_grad, key_acc, value_acc = state
            tile_keys, tile_values, tile_pos = tile_data(tile_id)
            scores, visible = scores_of(block_query, block_prefix, tile_keys, tile_pos)
            probs = jnp.where(
                visible, jnp.exp(scores - block_top[:, :, None]) / block_total[:, :, None], 0.0
            )
            dprobs = jnp.einsum(
                "qhd,khd->hqk", block_dout, tile_values, preferred_element_type=jnp.float32
            )
            dscores = (scaling * probs * (dprobs - block_inner[:, :, None])).astype(jnp.bfloat16)
            query_grad = query_grad + jnp.einsum(
                "hqk,khd->qhd", dscores, tile_keys, preferred_element_type=jnp.float32
            )
            offset = tile_id * key_tile
            key_term = jnp.einsum(
                "hqk,qhd->khd", dscores, block_query, preferred_element_type=jnp.float32
            )
            value_term = jnp.einsum(
                "hqk,qhd->khd",
                probs.astype(jnp.bfloat16),
                block_dout,
                preferred_element_type=jnp.float32,
            )
            key_acc = lax.dynamic_update_slice_in_dim(
                key_acc,
                lax.dynamic_slice_in_dim(key_acc, offset, key_tile, 0) + key_term,
                offset,
                0,
            )
            value_acc = lax.dynamic_update_slice_in_dim(
                value_acc,
                lax.dynamic_slice_in_dim(value_acc, offset, key_tile, 0) + value_term,
                offset,
                0,
            )
            return (query_grad, key_acc, value_acc)

        start_state = (jnp.zeros((query_tile, head_count, DH), jnp.float32), key_grad, value_grad)
        block_grad, key_grad, value_grad = sweep(block_id, update_grad, start_state)
        query_blocks.append(block_grad)
    query_part = jnp.concatenate(query_blocks, axis=0).reshape(latent_count, col_count)
    key_grads = key_grad.astype(jnp.bfloat16).reshape(row_count, col_count)
    value_grads = value_grad.astype(jnp.bfloat16).reshape(row_count, col_count)
    query_rows = lax.psum_scatter(query_part, "seq", scatter_dimension=0, tiled=True).astype(
        jnp.bfloat16
    )
    latent_rows = lax.dynamic_slice_in_dim(latents, seq_index * own_latents, own_latents, 0)
    latent_grad = lax.psum_scatter(
        jnp.dot(query_rows, query_weight.T, preferred_element_type=jnp.float32),
        "head",
        scatter_dimension=1,
        tiled=True,
    ).astype(jnp.bfloat16)
    query_weight_grad, key_weight_grad, value_weight_grad = (
        lax.psum_scatter(
            jnp.dot(latent_rows.T, query_rows, preferred_element_type=jnp.float32),
            "seq",
            scatter_dimension=0,
            tiled=True,
        ),
        lax.psum_scatter(
            jnp.dot(inputs.T, key_grads, preferred_element_type=jnp.float32),
            "seq",
            scatter_dimension=0,
            tiled=True,
        ),
        lax.psum_scatter(
            jnp.dot(inputs.T, value_grads, preferred_element_type=jnp.float32),
            "seq",
            scatter_dimension=0,
            tiled=True,
        ),
    )
    input_grad = lax.psum_scatter(
        jnp.dot(key_grads, key_weight.T, preferred_element_type=jnp.float32)
        + jnp.dot(value_grads, value_weight.T, preferred_element_type=jnp.float32),
        "head",
        scatter_dimension=0,
        tiled=True,
    ).astype(jnp.bfloat16)
    return (
        attention_out,
        input_grad,
        latent_grad,
        query_weight_grad,
        key_weight_grad,
        value_weight_grad,
        out_weight_grad,
    )


def solution(mesh):
    return jax.shard_map(
        on_device,
        mesh=mesh,
        in_specs=(
            P("seq", None),
            P(),
            P(None, "head"),
            P(None, "head"),
            P(None, "head"),
            P("head", None),
            P(),
            P("seq", "head"),
        ),
        out_specs=(
            P("seq", "head"),
            P(("seq", "head"), None),
            P("seq", "head"),
            P("seq", "head"),
            P("seq", "head"),
            P("seq", "head"),
            P("head", "seq"),
        ),
        check_vma=False,
    )
```

profile of v0, /device:TPU:0, one launch (start us, length us, event | category | flops | bytes accessed | tf_op | source)
XLA Modules:
  0.0 994.0 jit_solution(5352185387398604927)
XLA Ops:
  9.0 3.7 convolution_convert_fusion
  14.3 7.0 while.204
  21.4 7.5 while.205
  29.6 7.5 while.206
  37.9 7.5 while.207
  45.4 124.2 %pmax.7 = f32[4,2048]{1,0:T(4,128)S(1)} all-reduce(f32[4,2048]{1,0:T(4,128)S(1)} %pad_maximum_fusion.2), channel_id=1, replica_groups=mesh['seq'=32,'head'=4] {'seq'}, use_global_device_ids=true, to_apply=%region_22.23 | all-reduce | flops 8192 | bytes 65536 | tf_op jit(solution)/shard_map/pmax | solution.py:85
  172.3 12.0 %while.208 = (s32[]{:T(128)}, f32[4,512]{1,0:T(4,128)S(1)}, f32[512,4,64]{0,2,1:T(8,128)}, s32[4]{0:T(128)S(1)}, s32[2]{0:T(128)S(1)}, /*index=5*/s32[512]{0:T(5...) while((s32[]{:T(128)}, f32[4,512]{1,0:T(4,128)S(1)}, ...), condition=%wide.region_27.28_spmd.clone, body=%wide.region_23.27_spmd.clone.sunk | while | flops 277218304 | bytes 15274365 | solution.py:68
  173.6 4.7 conditional.40
  179.6 4.7 conditional.40
  185.2 14.4 %while.209 = (s32[]{:T(128)}, f32[4,512]{1,0:T(4,128)S(1)}, f32[512,4,64]{0,2,1:T(8,128)}, s32[4]{0:T(128)S(1)}, s32[2]{0:T(128)S(1)}, /*index=5*/s32[512]{0:T(5...) while((s32[]{:T(128)}, f32[4,512]{1,0:T(4,128)S(1)}, ...), condition=%wide.region_32.33_spmd.clone, body=%wide.region_28.32_spmd.clone.sunk | while | flops 277218304 | bytes 15274373 | solution.py:68
  187.6 4.7 conditional.41
  194.8 4.7 conditional.41
  200.4 14.4 %while.210 = (s32[]{:T(128)}, f32[4,512]{1,0:T(4,128)S(1)}, f32[512,4,64]{0,2,1:T(8,128)}, s32[4]{0:T(128)S(1)}, s32[2]{0:T(128)S(1)}, /*index=5*/s32[512]{0:T(5...) while((s32[]{:T(128)}, f32[4,512]{1,0:T(4,128)S(1)}, ...), condition=%wide.region_37.38_spmd.clone, body=%wide.region_33.37_spmd.clone.sunk | while | flops 277218304 | bytes 15274373 | solution.py:68
  202.9 4.7 conditional.42
  210.1 4.7 conditional.42
  215.7 12.5 %while.211 = (s32[]{:T(128)}, f32[4,512]{1,0:T(4,128)S(1)}, f32[512,4,64]{0,2,1:T(8,128)}, s32[4]{0:T(128)S(1)}, s32[2]{0:T(128)S(1)}, /*index=5*/s32[512]{0:T(5...) while((s32[]{:T(128)}, f32[4,512]{1,0:T(4,128)S(1)}, ...), condition=%wide.region_42.43_spmd.clone, body=%wide.region_38.42_spmd.clone.sunk | while | flops 277218304 | bytes 15274373 | solution.py:68
  218.2 3.8 conditional.43
  224.4 3.8 conditional.43
  228.8 3.0 pad_maximum_fusion
  231.8 2.9 copy.121
  234.8 13.3 %all_gather.6 = bf16[64,1024]{1,0:T(8,128)(2,1)S(1)} all-gather(bf16[64,256]{1,0:T(8,128)(2,1)S(1)} %copy-done.54), channel_id=1, replica_groups=mesh['seq'=32,'head'=4] {'head'}, dimensions={1}, use_global_device_ids=true | all-gather | bytes 163840 | tf_op jit(solution)/shard_map/all_gather | solution.py:129
  250.8 124.1 %psum.15 = f32[2048,4]{0,1:T(4,128)S(1)} all-reduce(f32[2048,4]{0,1:T(4,128)S(1)} %maximum_bitcast_fusion), channel_id=1, replica_groups=mesh['seq'=32,'head'=4] {'seq'}, use_global_device_ids=true, to_apply=%region_44.45 | all-reduce | flops 8192 | bytes 65536 | tf_op jit(solution)/shard_map/psum | solution.py:116
  376.5 2.9 copy.122
  379.5 5.2 all-gather.2.cloned.1.call-done
  384.7 4.7 convert_multiply_fusion
  389.4 3.0 copy.124
  398.9 18.0 %while.212 = (s32[]{:T(128)}, f32[512,4,64]{0,2,1:T(8,128)}, f32[1024,4,64]{0,2,1:T(8,128)S(1)}, f32[1024,4,64]{0,2,1:T(8,128)}, s32[4]{0:T(128)S(1)}, /*index=5...) while((s32[]{:T(128)}, f32[512,4,64]{0,2,1:T(8,128)}, ...), condition=%wide.region_50.0_spmd.clone, body=%wide.region_47.50_spmd.clone.sunk | while | flops 681182208 | bytes 42250848 | solution.py:68
  400.2 7.7 conditional.44
  409.2 7.7 conditional.44
  418.9 20.3 %while.213 = (s32[]{:T(128)}, f32[512,4,64]{0,2,1:T(8,128)}, f32[1024,4,64]{0,2,1:T(8,128)S(1)}, f32[1024,4,64]{0,2,1:T(8,128)}, s32[4]{0:T(128)S(1)}, /*index=5...) while((s32[]{:T(128)}, f32[512,4,64]{0,2,1:T(8,128)}, ...), condition=%wide.region_54.0_spmd.clone, body=%wide.region_51.54_spmd.clone.sunk | while | flops 681182208 | bytes 42250856 | solution.py:68
  421.4 7.7 conditional.45
  431.5 7.7 conditional.45
  441.2 20.4 %while.214 = (s32[]{:T(128)}, f32[512,4,64]{0,2,1:T(8,128)}, f32[1024,4,64]{0,2,1:T(8,128)S(1)}, f32[1024,4,64]{0,2,1:T(8,128)}, s32[4]{0:T(128)S(1)}, /*index=5...) while((s32[]{:T(128)}, f32[512,4,64]{0,2,1:T(8,128)}, ...), condition=%wide.region_58.0_spmd.clone, body=%wide.region_55.58_spmd.clone.sunk | while | flops 681182208 | bytes 42250856 | solution.py:68
  443.8 7.7 conditional.46
  453.9 7.7 conditional.46
  463.6 20.3 %while.215 = (s32[]{:T(128)}, f32[512,4,64]{0,2,1:T(8,128)}, f32[1024,4,64]{0,2,1:T(8,128)S(1)}, f32[1024,4,64]{0,2,1:T(8,128)}, s32[4]{0:T(128)S(1)}, /*index=5...) while((s32[]{:T(128)}, f32[512,4,64]{0,2,1:T(8,128)}, ...), condition=%wide.region_62.0_spmd.clone, body=%wide.region_59.62_spmd.clone.sunk | while | flops 681182208 | bytes 42250856 | solution.py:68
  466.1 7.7 conditional.47
  476.2 7.7 conditional.47
  483.9 3.0 pad_maximum_fusion.1
  486.9 2.9 copy.146
  492.9 74.5 %reduce-scatter.25.cloned.1.call-done = f32[64,256]{1,0:T(8,128)} async-done(((f32[2048,256]{1,0:T(8,128)}), f32[64,256]{1,0:T(8,128)}) %reduce-scatter.25.cloned.1.call-update) | async-done | bytes 65552
  573.3 2.8 convolution_add_fusion
  591.8 21.3 %reduce-scatter.19.cloned.1.call-done = f32[64,256]{1,0:T(8,128)} async-done(((f32[64,1024]{1,0:T(8,128)}), f32[64,256]{1,0:T(8,128)}) %reduce-scatter.19.cloned.1.call-update) | async-done | bytes 65552 | tf_op jit(solution)/shard_map/reduce_scatter | solution.py:215
  614.5 47.4 %reduce-scatter.17.cloned.1.call-done = f32[256,1024]{1,0:T(8,128)} async-done(((f32[1024,1024]{1,0:T(8,128)}), f32[256,1024]{1,0:T(8,128)}) %reduce-scatter.17.cloned.1.call-update) | async-done | bytes 1048592 | tf_op jit(solution)/shard_map/reduce_scatter | solution.py:241
  664.1 79.3 %reduce-scatter.27.cloned.1.call-done = f32[32,256]{1,0:T(8,128)} async-done(((f32[1024,256]{1,0:T(8,128)}), f32[32,256]{1,0:T(8,128)}) %reduce-scatter.27.cloned.1.call-update) | async-done | bytes 32784
  743.4 81.3 %reduce-scatter.29.cloned.1.call-done = f32[32,256]{1,0:T(8,128)} async-done(((f32[1024,256]{1,0:T(8,128)}), f32[32,256]{1,0:T(8,128)}) %reduce-scatter.29.cloned.1.call-update) | async-done | bytes 32784
  824.6 81.2 %reduce-scatter.23.cloned.1.call-done = f32[256,32]{0,1:T(8,128)} async-done(((f32[256,1024]{0,1:T(8,128)}), f32[256,32]{0,1:T(8,128)}) %reduce-scatter.23.cloned.1.call-update) | async-done | bytes 32784 | tf_op jit(solution)/shard_map/reduce_scatter | solution.py:133
  905.8 81.1 %reduce-scatter.21.cloned.1.call-done = f32[32,256]{1,0:T(8,128)} async-done(((f32[1024,256]{1,0:T(8,128)}), f32[32,256]{1,0:T(8,128)}) %reduce-scatter.21.cloned.1.call-update) | async-done | bytes 32784 | tf_op jit(solution)/shard_map/reduce_scatter | solution.py:222
  (488 shorter events, 199.9 us)
Async XLA Ops:
  7.2 6.3 copy-start
  7.2 372.3 %all-reduce.2.cloned.1.call-start = ((), (), s32[]{:S(2)}) async-start(), calls=%async_computation.8 | async-start | bytes 4194304 | tf_op jit(solution)/shard_map/psum | solution.py:116
  9.0 4.5 copy-start.51
  173.6 2.8 copy-start.39
  179.6 2.8 copy-start.39
  187.7 2.8 copy-start.41
  194.8 2.8 copy-start.41
  202.9 2.8 copy-start.43
  210.1 2.8 copy-start.43
  228.2 6.6 copy-start.10
  228.2 6.5 copy-start.15
  228.2 6.5 copy-start.28
  228.2 6.5 copy-start.49
  231.8 3.0 copy-start.54
  234.8 149.9 %all-gather.2.cloned.1.call-start = ((), (), s32[]{:S(2)}) async-start(), calls=%async_computation.10 | async-start | bytes 1081344 | tf_op jit(solution)/shard_map/all_gather | solution.py:139
  250.8 316.5 %reduce-scatter.25.cloned.1.call-start = ((), (), s32[]{:S(2)}) async-start(), calls=%async_computation.15 | async-start | bytes 2162688
  389.4 5.4 copy-start.38
  400.6 2.5 copy-start.16
  403.9 2.2 copy-start.1
  409.6 2.5 copy-start.16
  412.9 2.2 copy-start.1
  421.7 2.5 copy-start.17
  425.0 2.2 copy-start.3
  431.9 2.5 copy-start.17
  435.2 2.2 copy-start.3
  441.2 22.4 %copy-start.50 = (s32[512]{0:T(512)S(1)}, s32[512]{0:T(512)}, u32[]{:S(2)}) copy-start(s32[512]{0:T(512)} %copy-done.49) | copy-start | bytes 6148
  441.2 22.4 %copy-start.53 = (f32[4,512]{1,0:T(4,128)S(1)}, f32[4,512]{1,0:T(4,128)}, u32[]{:S(2)}) copy-start(f32[4,512]{1,0:T(4,128)} %get-tuple-element.4858) | copy-start | bytes 24580
  441.2 22.4 %copy-start.55 = (f32[4,512]{1,0:T(4,128)S(1)}, f32[4,512]{1,0:T(4,128)}, u32[]{:S(2)}) copy-start(f32[4,512]{1,0:T(4,128)} %get-tuple-element.4855) | copy-start | bytes 24580
  441.2 22.4 %copy-start.57 = (f32[4,512]{1,0:T(4,128)S(1)}, f32[4,512]{1,0:T(4,128)}, u32[]{:S(2)}) copy-start(f32[4,512]{1,0:T(4,128)} %copy-done.56) | copy-start | bytes 24580
  444.2 2.5 copy-start.18
  447.5 2.3 copy-start.5
  454.3 2.5 copy-start.18
  457.6 2.3 copy-start.5
  466.4 2.5 copy-start.19
  469.8 2.2 copy-start.7
  476.6 2.5 copy-start.19
  479.9 2.2 copy-start.7
  489.9 100.5 %reduce-scatter.15.cloned.1.call-start = ((), (), s32[]{:S(2)}) async-start(), calls=%async_computation.9 | async-start | bytes 327680 | tf_op jit(solution)/shard_map/reduce_scatter | solution.py:123
  491.9 121.1 %reduce-scatter.19.cloned.1.call-start = ((), (), s32[]{:S(2)}) async-start(), calls=%async_computation.12 | async-start | bytes 327680 | tf_op jit(solution)/shard_map/reduce_scatter | solution.py:215
  492.9 79.6 %copy-start.9 = (f32[1024,4,64]{0,2,1:T(8,128)S(1)}, f32[1024,4,64]{0,2,1:T(8,128)}, u32[]{:S(2)}) copy-start(f32[1024,4,64]{0,2,1:T(8,128)} %get-tuple-element.2774) | copy-start | bytes 3145732
  570.3 91.7 %reduce-scatter.17.cloned.1.call-start = ((), (), s32[]{:S(2)}) async-start(), calls=%async_computation.11 | async-start | bytes 5242880 | tf_op jit(solution)/shard_map/reduce_scatter | solution.py:241
  570.4 2.9 copy-start.52
  576.1 5.4 copy-start.37
  576.1 167.3 %reduce-scatter.27.cloned.1.call-start = ((), (), s32[]{:S(2)}) async-start(), calls=%async_computation.16 | async-start | bytes 1081344
  581.4 4.5 copy-start.48
  581.5 243.2 %reduce-scatter.29.cloned.1.call-start = ((), (), s32[]{:S(2)}) async-start(), calls=%async_computation.17 | async-start | bytes 1081344
  585.8 320.0 %reduce-scatter.23.cloned.1.call-start = ((), (), s32[]{:S(2)}) async-start(), calls=%async_computation.14 | async-start | bytes 1081344 | tf_op jit(solution)/shard_map/reduce_scatter | solution.py:133
  588.0 398.9 %reduce-scatter.21.cloned.1.call-start = ((), (), s32[]{:S(2)}) async-start(), calls=%async_computation.13 | async-start | bytes 1081344 | tf_op jit(solution)/shard_map/reduce_scatter | solution.py:222
  (56 other events, 63.9 us)
Sparse Core Ops, SparseCore 0:
  234.9 104.7 all-reduce.1
  342.5 42.1 all-gather.1
  490.0 77.2 reduce-scatter.24
  569.5 20.5 reduce-scatter.14
  592.3 20.6 reduce-scatter.18
  615.3 46.6 reduce-scatter.16
  666.0 77.2 reduce-scatter.26
  747.4 77.1 reduce-scatter.28
  828.7 77.0 reduce-scatter.22
  909.7 77.1 reduce-scatter.20
where the time goes:
time: 1000 us; the launch traced here: 994 us
  waiting for transfers between devices  471 us (47%)
  blocking collectives  262 us (26%)
  matrix products  103 us (10%)
  local copies, waits for them, and re-layouts  89.2 us (9%)
  loops' own time  29.6 us (3%)
  other arithmetic  24.2 us (2%)
  between operations  14.7 us (1%)
    unnamed x13, waiting for transfers between devices  235 us
    pmax x1, blocking collectives, on_device(): row_top = lax.pmax(jnp.concatenate(maxima, axis=1), 'seq')  124 us
    psum x1, blocking collectives, on_device(): exp_all, weighted_all = lax.psum((exp_total, weighted_sum), 'seq')  124 us
    reduce_scatter x1, waiting for transfers between devices, on_device(): lax.psum_scatter(jnp.dot(own_attended.T, grad_rows, preferred_element_typ...  81.2 us
    reduce_scatter x1, waiting for transfers between devices, on_device(): lax.psum_scatter(jnp.dot(latent_rows.T, query_rows, preferred_element_typ...  81.1 us
    reduce_scatter x1, waiting for transfers between devices, on_device(): lax.psum_scatter(jnp.dot(key_grads, key_weight.T, preferred_element_type=...  47.4 us
    dot_general x24, matrix products, scores_of(): jnp.einsum('qhd,khd->hqk', block_query, tile_keys, preferred_element_type...  46.7 us
    another operation x12, loops' own time, sweep(): return lax.fori_loop(0, tile_count, visit, init)  27.6 us
  transfers between devices with their start and end apart: 10, of which 8 were waited for; matrix products, arithmetic and copies ran while one was open for 4% of the time, Pallas kernels for 0%

commit v1 on v0

v1 whole, which is shorter than its diff:
```python
import functools

import jax
import jax.numpy as jnp
from jax import lax
from jax.experimental import pallas as pl
from jax.experimental.pallas import tpu as pltpu
from jax.sharding import PartitionSpec as P

MESH = pl.DeviceIdType.MESH
F32 = jnp.float32
BF16 = jnp.bfloat16
DH = 64
NS = 32
NC = 16
NZ = 4
NB = 8
QB = 256
KEYS = 1024
CH = 512
FLOOR = -1e30
LOG2E = 1.4426950408889634
(G, W, WF, A, AT, AF, OG, OS, L, SW, ZO, DG, ZK, ZV, LG, RC, RD, OC, SC, DC, A2) = (
    0, 1, 2, 3, 4, 5, 6, 7, 8, 9, 10, 11, 12, 13, 14, 15, 19, 24, 25, 26, 23)
NT = (((1,), (1,)), ((), ()))
TN = (((0,), (0,)), ((), ()))


def dotf(a, b, dims=None):
    if dims is None:
        return jnp.dot(a, b, preferred_element_type=F32)
    return lax.dot_general(a, b, dims, preferred_element_type=F32)


def each(low, high, body):
    def step(i, carry):
        body(i)
        return carry

    lax.fori_loop(low, high, step, 0)


def rows(i, n):
    return pl.ds(pl.multiple_of(i * n, n), n)


def mixed(pair, other, half):
    lane = lax.broadcasted_iota(jnp.int32, pair.shape, 1)
    keep = (lane < DH) if half == 0 else (lane >= DH)
    return jnp.where(keep, pair, other)


def split(value):
    high = value.astype(BF16).astype(F32)
    return jnp.concatenate([high, value - high], axis=0).astype(BF16)


def doubled(pair, half):
    return mixed(pair, pltpu.roll(pair, DH, 1), half).astype(BF16)


def half_mask(value, half):
    return mixed(value, jnp.zeros_like(value), half)


def shifted(me, d):
    x = (me // 8 + d // 8) % 4
    y = (me // 2 + d // 2) % 4
    return (x * 4 + y) * 2 + (me + d) % 2


def chip_ahead(chip, e):
    return ((chip // 4 + e // 4) % 4) * 4 + (chip + e) % 4


def chip_behind(chip, e):
    return ((chip // 4 + 4 - e // 4) % 4) * 4 + (chip + 16 - e) % 4


def offset_to(chip, target):
    return ((target // 4 + 4 - chip // 4) % 4) * 4 + (target + 16 - chip) % 4


def take(ref, sem):
    pltpu.make_async_copy(ref, ref, sem).wait()


def to_seq(src, dst, send, recv, j):
    return pltpu.make_async_remote_copy(
        src_ref=src, dst_ref=dst, send_sem=send, recv_sem=recv, device_id={"seq": j}, device_id_type=MESH)


def to_head(src, dst, send, recv, j):
    return pltpu.make_async_remote_copy(
        src_ref=src, dst_ref=dst, send_sem=send, recv_sem=recv, device_id={"head": j}, device_id_type=MESH)


def layer_kernel(
    x_h, lat_h, wq_h, wk_h, wv_h, wo_h, g_ref, pref_ref,
    ao_ref, ig_ref, lg_ref, dwq_ref, dwk_ref, dwv_ref, dwo_ref,
    x_v, lat_v, wq_v, w_all, wo_v, g4, q_v, qt_v, kz, vz, vt, kt, da_v, e_v, s_buf,
    ot_v, st_v, oc_v, sc_v, pre_v, prs_v, og_v, ogs_v, lrb, lrs, lr_v, att_v, att_s, aop, aor,
    dq_v, dqc, dqs, dqr, dqt, dkt, dsbuf, das, dav, sh_v, dq0, dv_acc, dk_v, dv_v, zk, zv, rp, rc, rs, rg, lgp, lgr,
    ld, snd, rcv, oc_r, sc_r, dc_r,
):
    me = lax.axis_index("seq")
    z = lax.axis_index("head")
    core = me % 2
    chip = me // 2
    twin = me + 1 - 2 * core
    base = me * KEYS

    def turn(i):
        near = i + 1
        mixed_up = jnp.where(i < 6, i + 2 - 2 * (i % 2), near)
        step = jnp.where(chip % 2 == 0, near, 32 - mixed_up)
        return (chip // 2 + step) % NB

    loads = [
        pltpu.make_async_copy(wk_h, w_all.at[0, z], ld.at[0]),
        pltpu.make_async_copy(wq_h, wq_v, ld.at[1]),
        pltpu.make_async_copy(lat_h, lat_v, ld.at[2]),
        pltpu.make_async_copy(wo_h, wo_v, ld.at[3]),
        pltpu.make_async_copy(wv_h, w_all.at[1, z], ld.at[4]),
    ]
    loads[0].start()
    for part in range(2):
        for r in range(4):
            pltpu.make_async_copy(
                x_h.at[r * 256 + part * 128:r * 256 + part * 128 + 128, :],
                x_v.at[part * CH + r * 128:part * CH + r * 128 + 128, :], ld.at[5]).start()
    for load in loads[1:]:
        load.start()
    barrier = pltpu.get_barrier_semaphore()

    @functools.partial(each, 1, NS)
    def _(d):
        pl.semaphore_signal(barrier, inc=1, device_id={"seq": shifted(me, d)}, device_id_type=MESH)

    for dz in range(1, NZ):
        pl.semaphore_signal(barrier, inc=1, device_id={"head": (z + dz) % NZ}, device_id_type=MESH)

    g4[z] = g_ref[...]
    row16 = lax.broadcasted_iota(jnp.int32, (16, KEYS), 0)
    ones = jnp.where(row16 == 0, 1.0, 0.0).astype(BF16)
    for h in range(4):
        vt[h, 64:80, :] = ones
    for p in range(2):
        for t in range(NC):
            st_v[p, t, 4:8, :] = jnp.zeros((4, 128), F32)
    loads[0].wait()
    take(x_v, ld.at[5])

    @functools.partial(each, 0, 2)
    def _(i):
        for j in range(2):
            at = rows(2 * i + j, 256)
            block = dotf(x_v[at, :], w_all[0, z]).astype(BF16).astype(F32)
            kt[:, at] = block.T.astype(BF16)
            for h in range(4):
                kz[h, at, :] = doubled(block[:, (h // 2) * 128:(h // 2) * 128 + 128], h % 2)

    loads[4].wait()

    @functools.partial(each, 0, 2)
    def _(i):
        for j in range(2):
            at = rows(2 * i + j, 256)
            block = dotf(x_v[at, :], w_all[1, z]).astype(BF16).astype(F32)
            flipped = block.T.astype(BF16)
            for h in range(4):
                vz[h, at, :] = doubled(block[:, (h // 2) * 128:(h // 2) * 128 + 128], h % 2)
                vt[h, 0:64, at] = flipped[h * 64:(h + 1) * 64, :]

    loads[1].wait()
    loads[2].wait()

    @functools.partial(each, 0, NB // 2)
    def _(i):
        for j in range(2):
            at = rows(2 * i + j, 256)
            block = (dotf(lat_v[at, :], wq_v[...]).astype(BF16).astype(F32) * 0.125)
            flipped = block.T
            qt_v[:, at] = flipped.astype(BF16)
            flipped = flipped * LOG2E
            for h in range(4):
                q_v[h, :, at] = split(flipped[h * 64:h * 64 + 64, :])

    pl.semaphore_wait(barrier, NS - 1 + NZ - 1)

    def g_copy(dz):
        return to_head(g_ref, g4.at[z], snd.at[G], rcv.at[G], (z + dz) % NZ)

    def w_copy(dz):
        return to_head(w_all.at[core, z], w_all.at[core, z], snd.at[W], rcv.at[W], (z + dz) % NZ)

    def wf_copy(dz):
        src = (z + NZ - dz) % NZ
        return to_seq(w_all.at[core, src], w_all.at[core, src], snd.at[WF], rcv.at[WF], twin)

    for dz in range(1, NZ):
        g_copy(dz).start()

    own_da = da_v.at[rows(me, 64), :]

    def a_first(k):
        t = chip_ahead(chip, jnp.where(core == 0, 4 * k, k))
        return to_seq(own_da, own_da, snd.at[A], rcv.at[A], 2 * t + core)

    def a_second(k, j):
        piece = da_v.at[rows(2 * chip_behind(chip, jnp.where(core == 0, 4 * j, j)) + core, 64), :]
        t = chip_ahead(chip, jnp.where(core == 0, k, 4 * k))
        return to_seq(piece, piece, snd.at[A2], rcv.at[A2], 2 * t + core)

    def a_twin():
        return to_seq(own_da, own_da, snd.at[AT], rcv.at[AT], twin)

    def af_copy(e):
        piece = da_v.at[rows(2 * chip_behind(chip, e) + core, 64), :]
        return to_seq(piece, piece, snd.at[AF], rcv.at[AF], twin)

    def own_cotangent():
        loads[3].wait()
        take(g4.at[0:3], rcv.at[G])
        acc = dotf(g4[0], wo_v[:, 0:256], NT)
        for i in range(1, NZ):
            acc = acc + dotf(g4[i], wo_v[:, i * 256:(i + 1) * 256], NT)
        da_v[rows(me, 64), :] = acc.astype(BF16)

    def send_cotangent():
        a_twin().start()

        for k in range(1, 4):
            a_first(k).start()

        for dz in range(1, NZ):
            w_copy(dz).start()

    def scores(b, h, slot, c):
        s = dotf(kz[h, c * CH:c * CH + CH, :], q_v[h, :, rows(b, QB)])
        pos = lax.broadcasted_iota(jnp.int32, (128, QB), 0)
        left = pref_ref[:, rows(b, QB)] - base - c * 128
        top = None
        for r in range(4):
            part = jnp.where(pos < left - r * 256, s[r * 128:r * 128 + 128, :], FLOOR)
            s_buf[slot, c * CH + r * 128:c * CH + r * 128 + 128, :] = part
            best = jnp.max(part, axis=0, keepdims=True)
            top = best if r == 0 else jnp.maximum(top, best)
        return top

    def oc_copy(b):
        pair = pl.ds(2 * b, 2)
        return to_seq(ot_v.at[1 - core, pair], oc_v.at[pair], snd.at[OC], oc_r.at[b], twin)

    def sc_copy(b):
        pair = pl.ds(2 * b, 2)
        return to_seq(st_v.at[1 - core, pair], sc_v.at[pair], snd.at[SC], sc_r.at[b], twin)

    def og_copy(t, e):
        return to_seq(pre_v.at[t], og_v.at[e], snd.at[OG], rcv.at[OG], 2 * t + core)

    def os_copy(t, e):
        return to_seq(prs_v.at[t], ogs_v.at[e], snd.at[OS], rcv.at[OS], 2 * t + core)

    def merge_out(b):
        oc_copy(b).wait_recv()
        sc_copy(b).wait_recv()
        for sub in range(2):
            t = 2 * b + sub
            mine = st_v[core, t]
            other = sc_v[t]
            top = jnp.maximum(mine, other)
            wa = jnp.exp2(mine - top)
            wb = jnp.exp2(other - top)
            prs_v[t, 0:2, :] = top[0:2, :]
            prs_v[t, 2:4, :] = wa[0:2, :] * mine[2:4, :] + wb[0:2, :] * other[2:4, :]
            prs_v[t, 4:8, :] = jnp.zeros((4, 128), F32)
            for half in range(2):
                cut = slice(half * 64, half * 64 + 64)
                pre_v[t, cut, :] = wa[half:half + 1, :] * ot_v[core, t, cut, :] + wb[half:half + 1, :] * oc_v[t, cut, :]
        for sub in range(2):
            t = 2 * b + sub
            e = offset_to(chip, t)

            @pl.when(e != 0)
            def _():
                og_copy(t, e).start()
                os_copy(t, e).start()

            @pl.when(e == 0)
            def _():
                og_v[0] = pre_v[t]
                ogs_v[0] = prs_v[t]

    def forward_block(i, m):
        b = turn(i)
        following = turn(i + 1)
        for h in range(4):
            p, half = h // 2, h % 2
            oz = None
            m_next = None
            for c in range(KEYS // CH):
                at = slice(c * CH, c * CH + CH)
                if h < 3:
                    part = scores(b, h + 1, (h + 1) % 2, c)
                else:
                    part = scores(following, 0, 0, c)
                m_next = part if c == 0 else jnp.maximum(m_next, part)
                e = jnp.exp2(s_buf[h % 2, at, :] - m).astype(BF16)
                e_v[b * 2 + p, at, half * QB:half * QB + QB] = e
                term = dotf(vt[h, :, at], e)
                oz = term if c == 0 else oz + term
            for sub in range(2):
                cut = slice(sub * 128, sub * 128 + 128)
                ot_v[p, 2 * b + sub, half * 64:half * 64 + 64, :] = oz[0:64, cut]
                st_v[p, 2 * b + sub, half:half + 1, :] = m[:, cut]
                st_v[p, 2 * b + sub, 2 + half:3 + half, :] = oz[64:65, cut]
            m = m_next
        oc_copy(b).start()
        sc_copy(b).start()

        @pl.when(i > 1)
        def _():
            merge_out(turn(i - 2))

        @pl.when(i == 4)
        def _():
            own_cotangent()

        @pl.when(i == 5)
        def _():
            send_cotangent()

        @pl.when(i == 7)
        def _():
            take(da_v.at[0:192, :], rcv.at[A])

            @functools.partial(each, 0, 4)
            def _(j):
                for k in range(1, 4):
                    a_second(k, j).start()

        return m

    start = None
    for c in range(KEYS // CH):
        part = scores(turn(0), 0, 0, c)
        start = part if c == 0 else jnp.maximum(start, part)
    lax.fori_loop(0, NB, forward_block, start)
    merge_out(turn(NB - 2))
    merge_out(turn(NB - 1))

    take(da_v.at[0:64, :], rcv.at[AT])
    take(og_v.at[1:NC], rcv.at[OG])
    take(ogs_v.at[1:NC], rcv.at[OS])
    stats = ogs_v[...]
    top = jnp.max(stats, axis=0, keepdims=True)
    weight = jnp.exp2(stats - top)
    sums = jnp.concatenate([stats[:, 2:8, :], stats[:, 0:2, :]], axis=1)
    total = jnp.sum(weight * sums, axis=0, keepdims=True)
    level = top[0] + jnp.log(total[0]) * LOG2E
    coef = weight / total
    halves = []
    for half in range(2):
        acc = jnp.zeros((64, 128), F32)
        for j in range(NC):
            acc = acc + coef[j, half:half + 1, :] * og_v[j, half * 64:half * 64 + 64, :]
        halves.append(acc.astype(BF16).astype(F32))
    attended_t = jnp.concatenate(halves, axis=0)
    da_t = da_v[rows(chip, 128), rows(core, 128)].astype(F32).T
    prod = da_t * attended_t
    lrs[0:2, :] = level[0:2, :]
    lrs[2:3, :] = jnp.sum(prod[0:64, :], axis=0, keepdims=True)
    lrs[3:4, :] = jnp.sum(prod[64:128, :], axis=0, keepdims=True)
    lrs[4:8, :] = jnp.zeros((4, 128), F32)
    lrb[me] = lrs[...]
    att_s[...] = attended_t.T.astype(BF16)

    def l_copy(d):
        return to_seq(lrs, lrb.at[me], snd.at[L], rcv.at[L], shifted(me, d))

    def at_copy():
        return to_seq(att_s.at[rows(1 - core, 64), :], att_v.at[core], snd.at[SW], rcv.at[SW], twin)

    for d in range(1, NS):
        l_copy(d).start()

    take(da_v.at[0:768, :], rcv.at[A2])

    for e in range(1, NC):
        af_copy(e).start()

    at_copy().start()
    att_v[core] = att_s[rows(core, 64), :]
    take(att_v.at[0], rcv.at[SW])
    attended = jnp.concatenate([att_v[0], att_v[1]], axis=1)
    for i in range(NZ):
        aop[i] = dotf(attended, wo_v[:, i * 256:(i + 1) * 256]).astype(BF16)
    for i in range(NZ):
        rp[0, 4 * i:4 * i + 4] = dotf(g4[i], attended, TN).astype(BF16).reshape(4, 2, 32, 256)

    def zo_copy(dz):
        t = (z + dz) % NZ
        return to_head(aop.at[t], aor.at[dz], snd.at[ZO], rcv.at[ZO], t)

    for dz in range(1, NZ):
        zo_copy(dz).start()

    def rc_copy(n):
        return to_seq(rp.at[n, :, 1 - core], rc.at[n], snd.at[RC + n], rcv.at[RC + n], twin)

    def rd_copy(n, e):
        t = chip_ahead(chip, e)
        return to_seq(rs.at[n, t], rg.at[n, e], snd.at[RD + n], rcv.at[RD + n], 2 * t + core)

    def reduce_mid(n):
        take(rc.at[n], rcv.at[RC + n])
        rs[n] = (rp[n, :, core].astype(F32) + rc[n].astype(F32)).astype(BF16)
        rg[n, 0] = rs[n, chip]

        for e in range(1, NC):
            rd_copy(n, e).start()

    def reduce_end(n):
        take(rg.at[n, 1:NC], rcv.at[RD + n])
        grad = rg[n, 0].astype(F32)
        for e in range(1, NC):
            grad = grad + rg[n, e].astype(F32)
        return grad

    rc_copy(0).start()
    dkt[...] = jnp.zeros_like(dkt)
    take(da_v.at[0:960, :], rcv.at[AF])
    take(lrb.at[0:NS - 1], rcv.at[L])
    for t in range(NC):
        lr_v[0:4, t * 128:(t + 1) * 128] = lrb[2 * t, 0:4, :]
        lr_v[4:8, t * 128:(t + 1) * 128] = lrb[2 * t + 1, 0:4, :]

    def dc_copy(b):
        pair = pl.ds(2 * b, 2)
        return to_seq(dq_v.at[pair, 1 - core], dqc.at[pair], snd.at[DC], dc_r.at[b], twin)

    def dg_copy(t, e):
        return to_seq(dqs.at[t], dqr.at[e], snd.at[DG], rcv.at[DG], 2 * t + core)

    def merge_dq(b):
        dc_copy(b).wait_recv()
        for sub in range(2):
            t = 2 * b + sub
            dqs[t] = (dq_v[t, core].astype(F32) + dqc[t].astype(F32)).astype(BF16)
        for sub in range(2):
            t = 2 * b + sub
            e = offset_to(chip, t)

            @pl.when(e != 0)
            def _():
                dg_copy(t, e).start()

            @pl.when(e == 0)
            def _():
                dqr[0] = dqs[t]

    @functools.partial(each, 0, NB)
    def _(b):
        at = rows(b, QB)
        da_t = da_v[at, :].astype(F32).T
        scaled = []
        for h in range(4):
            p, half = h // 2, h % 2
            local = jnp.concatenate([st_v[p, 2 * b], st_v[p, 2 * b + 1]], axis=1)[half:half + 1, :]
            factor = jnp.exp2(local - lr_v[4 * p + half:4 * p + half + 1, at])
            part = da_t[h * 64:h * 64 + 64, :] * factor
            das[h, :, at] = split(part)
            scaled.append(part)
            sh_v[h:h + 1, at] = lr_v[4 * p + 2 + half:4 * p + 3 + half, at] * factor
        da_s = jnp.concatenate(scaled, axis=0).T
        for p in range(2):
            pair = da_s[:, p * 128:(p + 1) * 128]
            for half in range(2):
                dav[p, rows(2 * b + half, QB), :] = half_mask(pair, half).astype(BF16)

    dv_acc[...] = jnp.zeros_like(dv_acc)

    def weight_term(n, grad_ref):
        @functools.partial(each, 0, 4)
        def _(i):
            term = dotf(x_v[:, rows(i, 256)], grad_ref[...], TN)
            rp[n, rows(i, 4)] = term.astype(BF16).reshape(4, 2, 32, 256)

        rc_copy(n).start()

    def cotangent(part, b, h):
        p, half = h // 2, h % 2
        span = slice(part * CH, part * CH + CH)
        at = rows(b, QB)
        dprob = (dotf(vz[h, span, :], das[h, :, at]) - sh_v[h:h + 1, at]).astype(BF16)
        dsbuf[half] = e_v[b * 2 + p, span, half * QB:half * QB + QB] * dprob

    def backward_block(part, i):
        b = turn(i)
        following = turn(i + 1)
        at = rows(b, QB)
        span = slice(part * CH, part * CH + CH)
        for h in range(4):
            cut = slice(h * 64, h * 64 + 64)
            p, half = h // 2, h % 2
            if h < 3:
                cotangent(part, b, h + 1)
            else:
                cotangent(part, following, 0)
            grad = dotf(kt[cut, span], dsbuf[half])
            if part == 0:
                dq0[b, cut, :] = grad
            else:
                dqt[cut, :] = dq0[b, cut, :] + grad
            dkt[cut, span] += dotf(qt_v[cut, at], dsbuf[half], NT)
            piece = slice(part * CH + half * (CH // 2), part * CH + (half + 1) * (CH // 2))
            dv_acc[piece, p * 128:(p + 1) * 128] += dotf(e_v[b * 2 + p, piece, :], dav[p, rows(b, 2 * QB), :])

    def zk_copy(part, dz):
        t = (z + dz) % NZ
        return to_head(dk_v.at[pl.ds(pl.multiple_of(part * CH + t * 128, 128), 128), :],
                       zk.at[dz, part * 128:part * 128 + 128], snd.at[ZK], rcv.at[ZK], t)

    def zv_copy(part, dz):
        t = (z + dz) % NZ
        return to_head(dv_v.at[pl.ds(pl.multiple_of(part * CH + t * 128, 128), 128), :],
                       zv.at[dz, part * 128:part * 128 + 128], snd.at[ZV], rcv.at[ZV], t)

    def half_done(part):
        span = slice(part * CH, part * CH + CH)
        dv_v[span, :] = dv_acc[span, :].astype(BF16)
        dk_v[span, :] = dkt[:, span].T.astype(BF16)
        own = pl.ds(pl.multiple_of(part * CH + z * 128, 128), 128)
        zk[0, part * 128:part * 128 + 128, :] = dk_v[own, :]
        zv[0, part * 128:part * 128 + 128, :] = dv_v[own, :]
        for dz in (2, 1, 3):
            zv_copy(part, dz).start()
            zk_copy(part, dz).start()

    cotangent(0, turn(0), 0)

    @functools.partial(each, 0, NB // 2)
    def _(i):
        backward_block(0, 2 * i)
        backward_block(0, 2 * i + 1)

        @pl.when(i == 0)
        def _():
            reduce_mid(0)

    half_done(0)
    cotangent(1, turn(0), 0)

    @functools.partial(each, 0, NB)
    def _(i):
        backward_block(1, i)
        b = turn(i)
        dq_v[pl.ds(2 * b, 2)] = (dqt[...].T * 0.125).astype(BF16).reshape(2, 2, 64, 256)
        dc_copy(b).start()

        @pl.when(i > 1)
        def _():
            merge_dq(turn(i - 2))

        @pl.when(i == 2)
        def _():
            take(w_all.at[0, 0:3], rcv.at[W])
            for dz in range(1, NZ):
                wf_copy(dz).start()

    half_done(1)
    merge_dq(turn(NB - 2))
    weight_term(1, dk_v)
    merge_dq(turn(NB - 1))
    weight_term(2, dv_v)
    reduce_mid(1)
    take(dqr.at[1:NC], rcv.at[DG])

    total = dqr[0].astype(F32)
    for e in range(1, NC):
        total = total + dqr[e].astype(F32)
    dq = total.astype(BF16)
    latents = lat_v[rows(me, 64), :]
    for i in range(4):
        term = dotf(latents[:, i * 256:(i + 1) * 256], dq, TN)
        rp[3, 4 * i:4 * i + 4] = term.astype(BF16).reshape(4, 2, 32, 256)
    rc_copy(3).start()
    for i in range(NZ):
        lgp[i] = dotf(dq, wq_v[i * 256:(i + 1) * 256, :], NT).astype(BF16)

    def lg_copy(dz):
        t = (z + dz) % NZ
        return to_head(lgp.at[t], lgr.at[dz], snd.at[LG], rcv.at[LG], t)

    for dz in range(1, NZ):
        lg_copy(dz).start()
    reduce_mid(2)
    reduce_mid(3)

    take(w_all.at[0, 0:3], rcv.at[WF])
    dwo_ref[...] = reduce_end(0)
    out = aop[z].astype(F32)
    take(aor.at[1:NZ], rcv.at[ZO])
    for dz in range(1, NZ):
        out = out + aor[dz].astype(F32)
    ao_ref[...] = out.astype(BF16)
    dwk_ref[...] = reduce_end(1)
    take(zv.at[1:NZ], rcv.at[ZV])
    take(zk.at[1:NZ], rcv.at[ZK])

    @functools.partial(each, 0, 4)
    def _(i):
        at = rows(i, 256)
        acc = jnp.zeros((256, 256), F32)
        for dz in range(NZ):
            src = (z + NZ - dz) % NZ
            acc = acc + dotf(zk[dz], w_all[0, src, at, :], NT) + dotf(zv[dz], w_all[1, src, at, :], NT)
        ig_ref[:, at] = acc.astype(BF16)

    grad = lgp[z].astype(F32)
    take(lgr.at[1:NZ], rcv.at[LG])
    for dz in range(1, NZ):
        grad = grad + lgr[dz].astype(F32)
    lg_ref[...] = grad.astype(BF16)
    dwv_ref[...] = reduce_end(2)
    dwq_ref[...] = reduce_end(3)

    take(g4.at[0:3], snd.at[G])
    take(w_all.at[0, 0:3], snd.at[W])
    take(w_all.at[0, 0:3], snd.at[WF])
    take(da_v.at[0:192, :], snd.at[A])
    take(da_v.at[0:768, :], snd.at[A2])
    take(da_v.at[0:64, :], snd.at[AT])
    take(da_v.at[0:960, :], snd.at[AF])
    take(og_v.at[1:NC], snd.at[OG])
    take(ogs_v.at[1:NC], snd.at[OS])
    take(lrb.at[0:NS - 1], snd.at[L])
    take(att_v.at[0], snd.at[SW])
    take(aor.at[1:NZ], snd.at[ZO])
    take(dqr.at[1:NC], snd.at[DG])
    take(zk.at[1:NZ], snd.at[ZK])
    take(zv.at[1:NZ], snd.at[ZV])
    take(lgr.at[1:NZ], snd.at[LG])
    take(oc_v, snd.at[OC])
    take(sc_v, snd.at[SC])
    take(dqc, snd.at[DC])
    for n in range(4):
        take(rc.at[n], snd.at[RC + n])
        take(rg.at[n, 1:NC], snd.at[RD + n])


def vspec():
    return pl.BlockSpec(memory_space=pltpu.VMEM)


def hspec():
    return pl.BlockSpec(memory_space=pl.ANY)


OUTS = (
    ((64, 256), BF16), ((256, 1024), BF16), ((64, 256), BF16),
    ((32, 256), F32), ((32, 256), F32), ((32, 256), F32), ((32, 256), F32),
)


def layer(x, lat, wq, wk, wv, wo, g, pref):
    sem = lambda *n: pltpu.SemaphoreType.DMA(n)
    b16 = lambda *n: pltpu.VMEM(n, BF16)
    f32 = lambda *n: pltpu.VMEM(n, F32)
    return pl.pallas_call(
        layer_kernel,
        name="layer",
        out_shape=tuple(jax.ShapeDtypeStruct(s, t) for s, t in OUTS),
        in_specs=[hspec()] * 6 + [vspec()] * 2,
        out_specs=tuple([vspec()] * 7),
        scratch_shapes=[
            b16(1024, 1024), b16(2048, 1024), b16(1024, 256), b16(2, NZ, 1024, 256), b16(256, 1024), b16(NZ, 64, 256),
            b16(4, 128, 2048), b16(256, 2048), b16(4, KEYS, 128), b16(4, KEYS, 128), b16(4, 80, KEYS), b16(256, KEYS),
            b16(2048, 256), b16(16, KEYS, 2 * QB), f32(2, KEYS, QB),
            f32(2, NC, 128, 128), f32(2, NC, 8, 128), f32(NC, 128, 128), f32(NC, 8, 128),
            f32(NC, 128, 128), f32(NC, 8, 128), f32(NC, 128, 128), f32(NC, 8, 128),
            f32(NS, 8, 128), f32(8, 128), f32(8, 2048), b16(2, 64, 128), b16(128, 128), b16(NZ, 64, 256), b16(NZ, 64, 256),
            b16(NC, 2, 64, 256), b16(NC, 64, 256), b16(NC, 64, 256), b16(NC, 64, 256),
            f32(256, QB), f32(256, KEYS), b16(2, CH, QB), b16(4, 128, 2048), b16(2, 4096, 128), f32(8, 2048), f32(NB, 256, QB), f32(KEYS, 256),
            b16(KEYS, 256), b16(KEYS, 256), b16(NZ, 256, 256), b16(NZ, 256, 256),
            b16(4, NC, 2, 32, 256), b16(4, NC, 32, 256), b16(4, NC, 32, 256), b16(4, NC, 32, 256),
            b16(NZ, 64, 256), b16(NZ, 64, 256),
            sem(6), sem(27), sem(24), sem(8), sem(8), sem(8),
        ],
        compiler_params=pltpu.CompilerParams(
            collective_id=0, has_side_effects=True, vmem_limit_bytes=66_000_000),
    )(x, lat, wq, wk, wv, wo, g, pref.reshape(1, 2048))


def finish_kernel(*refs):
    for i in range(7):
        refs[7 + i][...] = refs[i][...]


def finish(parts):
    return pl.pallas_call(
        finish_kernel,
        name="finish",
        out_shape=tuple(jax.ShapeDtypeStruct(s, t) for s, t in OUTS),
        in_specs=[vspec()] * 7,
        out_specs=tuple([vspec()] * 7),
    )(*parts)


def on_device(x, lat, wq, wk, wv, wo, pref, g):
    outs = finish(layer(x, lat, wq, wk, wv, wo, g, pref))
    return outs[:6] + (outs[6].T,)


def solution(mesh):
    return jax.shard_map(
        on_device,
        mesh=mesh,
        in_specs=(
            P("seq", None), P(), P(None, "head"), P(None, "head"), P(None, "head"), P("head", None), P(), P("seq", "head"),
        ),
        out_specs=(
            P("seq", "head"), P(("seq", "head"), None), P("seq", "head"), P("seq", "head"),
            P("seq", "head"), P("seq", "head"), P("head", "seq"),
        ),
        check_vma=False,
    )
```

time: 1000 us -> 83.6 us (0.08)
  waiting for transfers between devices: 471 us -> 0 us
  blocking collectives: 262 us -> 0 us
  matrix products: 103 us -> 0 us
  local copies, waits for them, and re-layouts: 89.2 us -> 0 us
  Pallas kernels: 0 us -> 82.8 us
  loops' own time: 29.6 us -> 0 us
  other arithmetic: 24.2 us -> 0 us
  between operations: 14.7 us -> 0.64 us
    unnamed x13 -> x0, waiting for transfers between devices: 235 us -> none
    reduce_scatter x5 -> x0, waiting for transfers between devices: 231 us -> none  [the longest x1 81.2 us: on_device(): lax.psum_scatter(jnp.dot(own_attended.T, grad_rows, preferred_element_typ...]
    pmax x1 -> x0, blocking collectives: 124 us -> none  [on_device(): row_top = lax.pmax(jnp.concatenate(maxima, axis=1), 'seq')]
    psum x1 -> x0, blocking collectives: 124 us -> none  [on_device(): exp_all, weighted_all = lax.psum((exp_total, weighted_sum), 'seq')]
    dot_general x76 -> x0, matrix products: 103 us -> none  [the longest x24 46.7 us: scores_of(): jnp.einsum('qhd,khd->hqk', block_query, tile_keys, preferred_element_type...]
    pallas_call x0 -> x2, Pallas kernels: none -> 82.8 us  [the longest x1 80.9 us: layer(): pl.pallas_call(layer_kernel, name='layer', out_shape=tuple((jax.ShapeDtyp...]
    another operation x36 -> x0, loops' own time: 29.6 us -> none  [the longest x12 27.6 us: sweep(): return lax.fori_loop(0, tile_count, visit, init)]
    cond x144 -> x0, local copies, waits for them, and re-layouts: 21.8 us -> none
  transfers between devices with their start and end apart: 10 -> 0, of which waited for: 8 -> 0; matrix products, arithmetic and copies ran while one was open for 4% -> 0% of each run, Pallas kernels for 0% -> 0%
where the time goes in v1:
time: 83.6 us; the launch traced here: 83.4 us
  Pallas kernels  82.8 us (99%)
    pallas_call x1, Pallas kernels, layer(): pl.pallas_call(layer_kernel, name='layer', out_shape=tuple((jax.ShapeDtyp...  80.9 us
    pallas_call x1, Pallas kernels, finish(): pl.pallas_call(finish_kernel, name='finish', out_shape=tuple((jax.ShapeDt...  1.93 us

profile of v1, /device:TPU:0, one launch (start us, length us, event | category | flops | bytes accessed | tf_op | source)
XLA Modules:
  0.0 83.4 jit_solution(11589927178192137767)
XLA Ops:
  0.6 80.9 %layer.1 = (bf16[64,256]{1,0:T(8,128)(2,1)}, bf16[256,1024]{1,0:T(8,128)(2,1)}, bf16[64,256]{1,0:T(8,128)(2,1)}, f32[32,256]{1,0:T(8,128)}, f32[32,256]{1,0:T(8,...) custom-call(bf16[1024,1024]{1,0:T(8,128)(2,1)} %x_h.1, bf16[2048,1024]{1,0:T(8,128)(2,1)} %lat_h.1, bf16[1024,256]{1,0:T(8,128)(2,1)} %wq_h.1, ...), custom_call_target="tpu_custom_call" | custom-call | tf_op jit(solution)/shard_map/layer/pallas_call | solution.py:671
  81.5 1.9 %finish.1 = (bf16[64,256]{1,0:T(8,128)(2,1)}, bf16[256,1024]{1,0:T(8,128)(2,1)}, bf16[64,256]{1,0:T(8,128)(2,1)}, f32[32,256]{1,0:T(8,128)}, f32[32,256]{1,0:T(8...) custom-call(bf16[64,256]{1,0:T(8,128)(2,1)} %get-tuple-element.21.refs_0_, bf16[256,1024]{1,0:T(8,128)(2,1)} %get-tuple-element.22.refs_1_, ...), custom_call_target="tpu_custom_call" | custom-call | tf_op jit(solution)/shard_map/finish/pallas_call | solution.py:702
